TPU v7x, 32 devices: a whole 2x2x4 slice. The times are simulated.
32 devices in a mesh: tile: 8 (over z, y), row: 4 (over x, core).
Axes of the slice: x: 2, y: 2, z: 4, core: 2. Of those that a mesh axis runs over, the one named last changes fastest.
Arguments:
- intensity: bfloat16 [8, 128, 11264], P('tile', 'row'), may hold values from 0.099609375 to 1
- volume: float32 [64, 128, 256], P('tile', 'row'), may hold values from 0 to 1
- footprint: bfloat16 [8, 256, 256], P('tile'), may hold values from 0.0010681152 to 0.021484375
- foot_offset: int32 [64, 8], replicated, may hold values from 2 to 84, as said below
- tile_count: int32 [8], replicated, may hold values from 1 to 8, as said below
Outputs:
- residual: float32 [8, 128, 11264], P('tile', 'row')
- correction: float32 [64, 128, 256], P('tile', 'row')
Inputs may be any that keep to these rules, and one draw needn't show every extreme that they name: `foot_offset`: slot j belongs to group j // 8. At every angle the offsets of one group's slots differ by at most 3; wherever a group has two or more slots, by exactly 3. `tile_count`: some group has all its slots live.
All inputs are finite; a program needn't handle non-finite values.
Results may differ from a plain program's by a relative error of at most 0.00065.
Values may be sent and summed in bfloat16 or wider, within the bound.
No kernel may reach another device: no remote copies, remote signals or barrier semaphores. Data moves between devices by JAX's collectives and lax.ppermute only.
A program may use at most 128 MiB of HBM per device.

v0:
```python
import jax
import jax.numpy as jnp
import numpy as np
from jax import lax
from jax.sharding import PartitionSpec as P

SPREAD = 4
RIM = 3
decay_length = 2.0
row_floor = 0.5


def with_halo(block, sides, width):
    for axis, dim in sides:
        count = lax.axis_size(axis)
        forward = [(i, i + 1) for i in range(count - 1)]
        backward = [(target, source) for source, target in forward]
        low = lax.ppermute(
            lax.slice_in_dim(block, block.shape[dim] - width, None, axis=dim), axis, forward
        )
        high = lax.ppermute(lax.slice_in_dim(block, 0, width, axis=dim), axis, backward)
        block = jnp.concatenate([low, block, high], axis=dim)
    return block


def smoothing_taps():
    spread_taps = np.exp(-np.abs(np.arange(-RIM, RIM + 1)) / decay_length)
    return spread_taps / spread_taps.sum()


def retrieve_phase(intensity):
    padded = with_halo(intensity, (("row", 1),), RIM)
    tap_weights = smoothing_taps()
    height_rows = intensity.shape[1]
    column_count = intensity.shape[2]
    across = float(tap_weights[0]) * padded[:, 0:height_rows, :].astype(jnp.float32)
    for tap_index in range(1, 2 * RIM + 1):
        across = across + float(tap_weights[tap_index]) * padded[
            :, tap_index : tap_index + height_rows, :
        ].astype(jnp.float32)
    widened = jnp.pad(across, ((0, 0), (0, 0), (RIM, RIM)))
    smoothed = float(tap_weights[0]) * widened[:, :, 0:column_count]
    for tap_index in range(1, 2 * RIM + 1):
        smoothed = (
            smoothed
            + float(tap_weights[tap_index]) * widened[:, :, tap_index : tap_index + column_count]
        )
    return -jnp.log(smoothed)


def live_flags(tile_count, slots_here):
    group_total = tile_count.shape[0]
    slot_ids = jnp.arange(group_total * slots_here, dtype=jnp.int32)
    repeated = jnp.broadcast_to(tile_count[:, None], (group_total, slots_here)).reshape(-1)
    return (slot_ids % slots_here < repeated).astype(jnp.float32)


def row_totals(footprint, offsets_here, live_all, block_count):
    half_cols = footprint.shape[2] // 2
    block_ids = jnp.arange(block_count, dtype=jnp.int32)
    matches = (offsets_here[:, :, None] == block_ids[None, None, :]).astype(jnp.float32)
    counts = jnp.sum(matches * live_all[:, None, None], axis=0)
    voxel_sums = jnp.sum(footprint, axis=1, dtype=jnp.float32)
    leading = counts[:, :, None] * voxel_sums[:, None, :half_cols]
    trailing = counts[:, :, None] * voxel_sums[:, None, half_cols:]
    trailing = jnp.concatenate([jnp.zeros_like(trailing[:, :1]), trailing[:, :-1]], axis=1)
    return (leading + trailing).reshape(counts.shape[0], -1)


def project_loads(load_half, footprint):
    half_cols = footprint.shape[2] // 2
    images = jnp.einsum("abrv,avc->arbc", load_half, footprint, preferred_element_type=jnp.float32)
    leading = images[..., :half_cols]
    trailing = images[..., half_cols:]
    trailing = jnp.concatenate([jnp.zeros_like(trailing[:, :, :1]), trailing[:, :, :-1]], axis=2)
    joined = leading + trailing
    return joined.reshape(joined.shape[0], joined.shape[1], -1)


def back_project(weighted, footprint):
    half_cols = footprint.shape[2] // 2
    halves = weighted.reshape(weighted.shape[0], weighted.shape[1], -1, half_cols)
    nearer = jnp.einsum(
        "arbc,avc->abrv", halves, footprint[:, :, :half_cols], preferred_element_type=jnp.float32
    )
    farther = jnp.einsum(
        "arbc,avc->abrv", halves, footprint[:, :, half_cols:], preferred_element_type=jnp.float32
    )
    farther = jnp.concatenate([farther[:, 1:], jnp.zeros_like(farther[:, :1])], axis=1)
    return nearer + farther


def local(intensity, volume, footprint, foot_offset, tile_count):
    phase_map = retrieve_phase(intensity)
    slots_here = volume.shape[0]
    angles_here = footprint.shape[0]
    half_cols = footprint.shape[2] // 2
    block_count = intensity.shape[2] // half_cols
    member = lax.axis_index("tile")
    live_all = live_flags(tile_count, slots_here)
    live_mine = lax.dynamic_slice_in_dim(live_all, member * slots_here, slots_here)
    masked = volume * live_mine[:, None, None]
    offsets_here = lax.dynamic_slice_in_dim(foot_offset, member * angles_here, angles_here, 1)
    column_sums = lax.psum(jnp.sum(footprint, axis=(0, 2), dtype=jnp.float32), "tile")
    row_sums = row_totals(footprint, offsets_here, live_all, block_count)
    group_total = tile_count.shape[0]
    grouped = foot_offset.reshape(group_total, slots_here, -1)
    starts = jnp.min(grouped, axis=1)
    deltas = lax.dynamic_slice_in_dim(grouped, member, 1, 0)[0] - lax.dynamic_slice_in_dim(
        starts, member, 1, 0
    )
    places = jnp.arange(SPREAD, dtype=jnp.int32)
    picked = (deltas[:, :, None] == places[None, None, :]).astype(jnp.float32)
    outgoing = jnp.einsum("jas,jrv->asrv", picked, masked, precision=lax.Precision.HIGHEST)
    arrived = lax.all_to_all(
        outgoing.astype(jnp.bfloat16), "tile", split_axis=0, concat_axis=1, tiled=True
    ).astype(outgoing.dtype)
    starts_here = lax.dynamic_slice_in_dim(starts, member * angles_here, angles_here, 1)
    targets = (jnp.transpose(starts_here)[:, :, None] + places[None, None, :]).reshape(
        angles_here, -1
    )
    load_blocks = jnp.stack([jax.ops.segment_sum(arrived[0], targets[0], num_segments=block_count)])
    projection = project_loads(load_blocks.astype(jnp.bfloat16), footprint)
    residual = phase_map - projection
    weighted = (residual / jnp.maximum(row_sums, row_floor)[:, None, :]).astype(jnp.bfloat16)
    back_blocks = back_project(weighted, footprint)
    returned = jnp.stack([jnp.take(back_blocks[0], targets[0], axis=0)])
    received = lax.all_to_all(returned, "tile", split_axis=1, concat_axis=0, tiled=True)
    summed = jnp.einsum("jas,asrv->jrv", picked, received, precision=lax.Precision.HIGHEST)
    correction = summed * live_mine[:, None, None] / column_sums[None, None, :]
    return (residual, correction)


def solution(mesh):
    placed = (P("tile", "row", None), P("tile", "row", None), P("tile", None, None), P(), P())
    return jax.shard_map(
        local,
        mesh=mesh,
        in_specs=placed,
        out_specs=(P("tile", "row", None), P("tile", "row", None)),
        check_vma=False,
    )
```

profile of v0, /device:TPU:8, one launch (start us, length us, event | category | flops | bytes accessed | tf_op | source)
XLA Modules:
  0.0 82.8 jit_solution(16312274930662407107)
XLA Ops:
  0.6 0.7 broadcast_in_dim.12
  1.4 0.1 reshape.331
  1.4 0.8 copy.69
  2.2 0.1 dynamic_slice.23
  2.3 1.7 %convolution_convert_fusion = bf16[8,4,32,256]{3,0,2,1:T(8,128)(2,1)S(1)} fusion(f32[8,32,256]{2,1,0:T(8,128)} %param.6, f32[8]{0:T(128)S(1)} %dynamic_slice.23, s32[8,8]{1,0:T(8,128)S(1)} %bitcast_subtract_fusion), kind=kOutput, calls=%fused_computation.16 | convolution fusion | flops 25493760 | bytes 786720 | tf_op jit(solution)/shard_map/jas,jrv->asrv/dot_general | solution.py:114
  4.0 0.9 %copy.72 = bf16[8,4,32,256]{3,2,1,0:T(8,128)(2,1)} copy(bf16[8,4,32,256]{3,0,2,1:T(8,128)(2,1)S(1)} %convolution_convert_fusion) | data formatting | bytes 1048576 | tf_op jit(solution)/shard_map/convert_element_type | solution.py:116
  4.9 6.4 %all-to-all-start = ((bf16[8,4,32,256]{3,2,1,0:T(8,128)(2,1)}), bf16[8,4,32,256]{3,2,1,0:T(8,128)(2,1)S(1)}, u32[]{:S(2)}, u32[]{:S(2)}) async-start(bf16[8,4,32,256]{3,2,1,0:T(8,128)(2,1)} %copy.72), calls=%async_computation | async-start | bytes 1048576 | tf_op jit(solution)/shard_map/all_to_all | solution.py:115
  11.3 0.1 fusion.28
  11.4 1.3 %collective-permute-start = (bf16[1,3,11264]{2,1,0:T(4,128)(2,1)S(1)}, bf16[1,3,11264]{2,1,0:T(4,128)(2,1)S(1)}, u32[]{:S(2)}, u32[]{:S(2)}) collective-permute-start(bf16[1,3,11264]{2,1,0:T(4,128)(2,1)S(1)} %get-tuple-element.19), channel_id=1, source_target_pairs={{0,1},{1,2},{2,3},{4,5},{5,6},{6,7},{8,9},{9,10},{10,11},{12,13},{... | collective-permute-start | bytes 202760 | tf_op jit(solution)/shard_map/ppermute | solution.py:18
  12.7 1.3 %collective-permute-start.1 = (bf16[1,3,11264]{2,1,0:T(4,128)(2,1)S(1)}, bf16[1,3,11264]{2,1,0:T(4,128)(2,1)S(1)}, u32[]{:S(2)}, u32[]{:S(2)}) collective-permute-start(bf16[1,3,11264]{2,1,0:T(4,128)(2,1)S(1)} %get-tuple-element.18), channel_id=1, source_target_pairs={{1,0},{2,1},{3,2},{5,4},{6,5},{7,6},{9,8},{10,9},{11,10},{13,12},{... | collective-permute-start | bytes 202760 | tf_op jit(solution)/shard_map/ppermute | solution.py:21
  14.0 0.7 fusion.26
  14.7 0.2 dynamic-slice_reduce_fusion
  14.9 0.1 add.151
  15.0 0.1 add.152
  15.1 0.1 add.159
  15.2 0.1 convert_reduce_fusion
  15.3 0.1 select_reduce_fusion
  15.4 0.1 add.154
  15.5 0.1 add.161
  15.6 0.1 broadcast_multiply_fusion
  15.7 0.1 maximum_bitcast_fusion
  15.8 1.8 %collective-permute-done.1 = bf16[1,3,11264]{2,1,0:T(4,128)(2,1)S(1)} collective-permute-done((bf16[1,3,11264]{2,1,0:T(4,128)(2,1)S(1)}, bf16[1,3,11264]{2,1,0:T(4,128)(2,1)S(1)}, u32[]{:S(2)}, u32[]{:S(2)}) %collective-permute-start.1) | collective-permute-done | bytes 67616 | tf_op jit(solution)/shard_map/ppermute | solution.py:21
  17.6 0.1 constant_dynamic-update-slice_fusion
  17.7 0.0 collective-permute-done
  17.7 2.5 %multiply_add_fusion = f32[1,32,11264]{2,1,0:T(8,128)} fusion(bf16[1,32,11264]{2,1,0:T(8,128)(2,1)S(1)} %copy-done.1, bf16[1,3,11264]{2,1,0:T(4,128)(2,1)S(1)} %collective-permute-done, bf16[1,35,11264]{2,1,0:T(8,128)(2,1)S(1)} %constant_dynamic-update-slice_fusion), kind=kLoop, calls=%fused_computation.15 | loop fusion | flops 10452992 | bytes 4392960 | tf_op jit(solution)/shard_map/add | solution.py:38
  20.2 4.4 %all-to-all-done = bf16[8,4,32,256]{3,2,1,0:T(8,128)(2,1)S(1)} async-done(((bf16[8,4,32,256]{3,2,1,0:T(8,128)(2,1)}), bf16[8,4,32,256]{3,2,1,0:T(8,128)(2,1)S(1)}, u32[]{:S(2)}, u32[]{:S(2)}) %all-to-all-start) | async-done | bytes 524320 | tf_op jit(solution)/shard_map/all_to_all | solution.py:115
  24.6 1.1 %bitcast_convert_fusion = f32[32,32,256]{2,1,0:T(8,128)} fusion(bf16[8,4,32,256]{3,2,1,0:T(8,128)(2,1)S(1)} %all-to-all-done), kind=kLoop, calls=%fused_computation.31 | loop fusion | flops 262144 | bytes 1572864 | tf_op jit(solution)/shard_map/convert_element_type | solution.py:117
  25.7 0.3 broadcast_in_dim.11
  26.0 3.8 %scatter_fusion = f32[88,32,256]{2,1,0:T(8,128)S(1)} fusion(f32[88,32,256]{2,1,0:T(8,128)S(1)} %broadcast_in_dim.11, s32[32]{0:T(128)S(1)} %get-tuple-element.21, f32[32,32,256]{2,1,0:T(8,128)} %bitcast_convert_fusion), kind=kCustom, calls=%fused_computation.1 | custom fusion | flops 262144 | bytes 3145856 | tf_op jit(solution)/shard_map/scatter-add | solution.py:122
  29.8 0.5 convolution_bitcast_fusion.1
  30.4 0.1 slice.107
  30.5 0.2 slice_add_fusion
  30.7 0.0 copy-start
  30.8 0.8 %copy.73 = f32[1,32,88,128]{3,2,0,1:T(8,128)S(1)} copy(f32[1,32,88,128]{3,1,2,0:T(8,128)S(1)} %slice_add_fusion) | data formatting | bytes 2883584 | tf_op jit(solution)/shard_map/add | solution.py:76
  31.6 0.5 copy-done
  32.1 3.4 %fusion.11 = (bf16[4,8,88,128]{3,1,2,0:T(8,128)(2,1)S(1)}, f32[1,32,11264]{2,1,0:T(8,128)}) fusion(f32[11264]{0:T(1024)S(1)} %maximum_bitcast_fusion, f32[1,32,11264]{2,0,1:T(1,128)S(1)} %bitcast.95, f32[1,32,11264]{2,1,0:T(8,128)S(1)} %copy-done), kind=kLoop, calls=%fused_computation.30 | loop fusion | flops 6127616 | bytes 5091328
  35.5 0.1 copy.83
  35.6 0.6 convolution_bitcast_fusion
  36.2 0.2 slice.111
  36.4 0.6 fusion
  37.0 0.9 %copy.75 = f32[88,32,256]{2,1,0:T(8,128)S(1)} copy(f32[88,32,256]{2,0,1:T(8,128)S(1)} %fusion) | data formatting | bytes 5767168 | tf_op jit(solution)/shard_map/squeeze | solution.py:127
  37.9 1.6 %gather_fusion = f32[32,32,256]{2,1,0:T(8,128)} fusion(f32[88,32,256]{2,1,0:T(8,128)S(1)} %copy.75, s32[1024]{0:T(1024)S(1)} %pad_clamp_fusion), kind=kCustom, calls=%fused_computation | custom fusion | bytes 2097280 | tf_op jit(solution)/shard_map/jit(_take)/gather | solution.py:127
  39.5 2.4 %fusion.7 = f32[1,32,32,256]{3,2,0,1:T(8,128)} fusion(f32[32,32,256]{2,1,0:T(8,128)} %gather_fusion, pred[32]{0:T(512)(128)(4,1)S(1)} %compare_and_fusion), kind=kLoop, calls=%fused_computation.23 | loop fusion | flops 262144 | bytes 2097184 | tf_op jit(solution)/shard_map/jit(_take)/select_n | solution.py:127
  41.9 4.9 %all-to-all-start.1 = ((f32[1,32,32,256]{3,2,0,1:T(8,128)}), f32[1,32,32,256]{3,2,0,1:T(8,128)S(1)}, u32[]{:S(2)}, u32[]{:S(2)}) async-start(f32[1,32,32,256]{3,2,0,1:T(8,128)} %fusion.7), calls=%async_computation.1 | async-start | bytes 2097152 | tf_op jit(solution)/shard_map/all_to_all | solution.py:128
  46.8 33.8 %psum.7 = f32[256]{0:T(256)S(1)} all-reduce(f32[256]{0:T(256)S(1)} %get-tuple-element.14), channel_id=1, replica_groups=mesh['tile'=8,'row'=4] {'tile'}, use_global_device_ids=true, to_apply=%region_5.6 | all-reduce | flops 256 | bytes 2048 | tf_op jit(solution)/shard_map/psum | solution.py:104
  80.5 0.0 all-to-all-done.1
  80.5 1.5 %fusion.6 = f32[8,32,256]{2,0,1:T(8,128)S(1)} fusion(f32[8,4,32,256]{3,2,1,0:T(8,128)S(1)} %bitcast.96, f32[256]{0:T(256)S(1)} %psum.7, f32[8]{0:T(128)S(1)} %dynamic_slice.23, s32[8,8]{1,0:T(8,128)S(1)} %bitcast_subtract_fusion), kind=kOutput, calls=%fused_computation.21 | convolution fusion | flops 25297152 | bytes 1312032 | tf_op jit(solution)/shard_map/jas,asrv->jrv/dot_general | solution.py:129
  82.0 0.8 copy.78
  (15 shorter events, 0.1 us)
Async XLA Ops:
  2.3 9.0 %copy-start.1 = (bf16[1,32,11264]{2,1,0:T(8,128)(2,1)S(1)}, bf16[1,32,11264]{2,1,0:T(8,128)(2,1)}, u32[]{:S(2)}) copy-start(bf16[1,32,11264]{2,1,0:T(8,128)(2,1)} %param.5) | copy-start | bytes 2162692
  4.9 10.3 %copy-start.2 = (bf16[1,256,256]{2,1,0:T(8,128)(2,1)S(1)}, bf16[1,256,256]{2,1,0:T(8,128)(2,1)}, u32[]{:S(2)}) copy-start(bf16[1,256,256]{2,1,0:T(8,128)(2,1)} %param.7) | copy-start | bytes 393220
  4.9 19.6 %all-to-all-start = ((bf16[8,4,32,256]{3,2,1,0:T(8,128)(2,1)}), bf16[8,4,32,256]{3,2,1,0:T(8,128)(2,1)S(1)}, u32[]{:S(2)}, u32[]{:S(2)}) async-start(bf16[8,4,32,256]{3,2,1,0:T(8,128)(2,1)} %copy.72), calls=%async_computation | async-start | bytes 1048576 | tf_op jit(solution)/shard_map/all_to_all | solution.py:115
  11.4 6.3 %collective-permute-start = (bf16[1,3,11264]{2,1,0:T(4,128)(2,1)S(1)}, bf16[1,3,11264]{2,1,0:T(4,128)(2,1)S(1)}, u32[]{:S(2)}, u32[]{:S(2)}) collective-permute-start(bf16[1,3,11264]{2,1,0:T(4,128)(2,1)S(1)} %get-tuple-element.19), channel_id=1, source_target_pairs={{0,1},{1,2},{2,3},{4,5},{5,6},{6,7},{8,9},{9,10},{10,11},{12,13},{... | collective-permute-start | bytes 202760 | tf_op jit(solution)/shard_map/ppermute | solution.py:18
  12.7 4.9 %collective-permute-start.1 = (bf16[1,3,11264]{2,1,0:T(4,128)(2,1)S(1)}, bf16[1,3,11264]{2,1,0:T(4,128)(2,1)S(1)}, u32[]{:S(2)}, u32[]{:S(2)}) collective-permute-start(bf16[1,3,11264]{2,1,0:T(4,128)(2,1)S(1)} %get-tuple-element.18), channel_id=1, source_target_pairs={{1,0},{2,1},{3,2},{5,4},{6,5},{7,6},{9,8},{10,9},{11,10},{13,12},{... | collective-permute-start | bytes 202760 | tf_op jit(solution)/shard_map/ppermute | solution.py:21
  30.7 1.4 %copy-start = (f32[1,32,11264]{2,1,0:T(8,128)S(1)}, f32[1,32,11264]{2,1,0:T(8,128)}, u32[]{:S(2)}) copy-start(f32[1,32,11264]{2,1,0:T(8,128)} %multiply_add_fusion) | copy-start | bytes 4325380
  41.9 38.7 %all-to-all-start.1 = ((f32[1,32,32,256]{3,2,0,1:T(8,128)}), f32[1,32,32,256]{3,2,0,1:T(8,128)S(1)}, u32[]{:S(2)}, u32[]{:S(2)}) async-start(f32[1,32,32,256]{3,2,0,1:T(8,128)} %fusion.7), calls=%async_computation.1 | async-start | bytes 2097152 | tf_op jit(solution)/shard_map/all_to_all | solution.py:128
where the time goes:
time: 83.4 us; the launch traced here: 82.8 us
  blocking collectives  33.8 us (41%)
  starting transfers between devices  13.9 us (17%)
  other arithmetic  13.8 us (17%)
  local copies, waits for them, and re-layouts  9.5 us (11%)
  waiting for transfers between devices  6.21 us (7%)
  matrix products  4.79 us (6%)
  between operations  0.84 us (1%)
    psum x1, blocking collectives, local(): lax.psum(jnp.sum(footprint, axis=(0, 2), dtype=jnp.float32), 'tile')  33.8 us
    all_to_all x1, starting transfers between devices, local(): lax.all_to_all(outgoing.astype(jnp.bfloat16), 'tile', split_axis=0, conca...  6.41 us
    all_to_all x1, starting transfers between devices, local(): lax.all_to_all(returned, 'tile', split_axis=1, concat_axis=0, tiled=True)  4.9 us
    all_to_all x1, waiting for transfers between devices, local(): lax.all_to_all(outgoing.astype(jnp.bfloat16), 'tile', split_axis=0, conca...  4.39 us
    scatter-add x1, other arithmetic, local(): jax.ops.segment_sum(arrived[0], targets[0], num_segments=block_count)  3.78 us
    unnamed x1, other arithmetic  3.4 us
    add x1, other arithmetic, retrieve_phase(): across + float(tap_weights[tap_index]) * padded[:, tap_index:tap_index +...  2.47 us
    select_n x2, other arithmetic, local(): returned = jnp.stack([jnp.take(back_blocks[0], targets[0], axis=0)])  2.36 us
  transfers between devices with their start and end apart: 4, of which 2 were waited for; matrix products, arithmetic and copies ran while one was open for 5% of the time, Pallas kernels for 0%

commit v1 on v0

--- a/solution.py
+++ b/solution.py
@@ -91,6 +91,11 @@
 
 
 def local(intensity, volume, footprint, foot_offset, tile_count):
+
+    def quotas_register(s0):
+        arr_next = jnp.sum(lax.all_gather(s0, axis_name="tile"), axis=0)
+        return arr_next
+
     phase_map = retrieve_phase(intensity)
     slots_here = volume.shape[0]
     angles_here = footprint.shape[0]
@@ -101,7 +106,7 @@
     live_mine = lax.dynamic_slice_in_dim(live_all, member * slots_here, slots_here)
     masked = volume * live_mine[:, None, None]
     offsets_here = lax.dynamic_slice_in_dim(foot_offset, member * angles_here, angles_here, 1)
-    column_sums = lax.psum(jnp.sum(footprint, axis=(0, 2), dtype=jnp.float32), "tile")
+    column_sums = quotas_register(jnp.sum(footprint, axis=(0, 2), dtype=jnp.float32))
     row_sums = row_totals(footprint, offsets_here, live_all, block_count)
     group_total = tile_count.shape[0]
     grouped = foot_offset.reshape(group_total, slots_here, -1)

time: 83.4 us -> 83.2 us (level)
    psum x1 -> x0, blocking collectives: 33.8 us -> none  [local(): lax.psum(jnp.sum(footprint, axis=(0, 2), dtype=jnp.float32), 'tile')]
    all_gather x0 -> x1, blocking collectives: none -> 33.5 us  [quotas_register(): arr_next = jnp.sum(lax.all_gather(s0, axis_name='tile'), axis=0)]
where the time goes in v1:
time: 83.2 us; the launch traced here: 82.6 us
  blocking collectives  33.5 us (40%)
  starting transfers between devices  13.9 us (17%)
  other arithmetic  13.8 us (17%)
  local copies, waits for them, and re-layouts  9.5 us (11%)
  waiting for transfers between devices  6.21 us (7%)
  matrix products  4.79 us (6%)
  between operations  0.84 us (1%)
    all_gather x1, blocking collectives, quotas_register(): arr_next = jnp.sum(lax.all_gather(s0, axis_name='tile'), axis=0)  33.5 us
    all_to_all x1, starting transfers between devices, local(): lax.all_to_all(outgoing.astype(jnp.bfloat16), 'tile', split_axis=0, conca...  6.41 us
    all_to_all x1, starting transfers between devices, local(): lax.all_to_all(returned, 'tile', split_axis=1, concat_axis=0, tiled=True)  4.9 us
    all_to_all x1, waiting for transfers between devices, local(): lax.all_to_all(outgoing.astype(jnp.bfloat16), 'tile', split_axis=0, conca...  4.39 us
    scatter-add x1, other arithmetic, local(): jax.ops.segment_sum(arrived[0], targets[0], num_segments=block_count)  3.78 us
    unnamed x1, other arithmetic  3.4 us
    add x1, other arithmetic, retrieve_phase(): across + float(tap_weights[tap_index]) * padded[:, tap_index:tap_index +...  2.47 us
    select_n x2, other arithmetic, local(): returned = jnp.stack([jnp.take(back_blocks[0], targets[0], axis=0)])  2.36 us
  transfers between devices with their start and end apart: 4, of which 2 were waited for; matrix products, arithmetic and copies ran while one was open for 5% of the time, Pallas kernels for 0%

profile of v1, /device:TPU:8, one launch (start us, length us, event | category | flops | bytes accessed | tf_op | source)
XLA Modules:
  0.0 82.6 jit_solution(4081496611962584144)
XLA Ops:
  0.6 0.7 broadcast_in_dim.12
  1.4 0.1 reshape.331
  1.4 0.8 copy.69
  2.2 0.1 dynamic_slice.23
  2.3 1.7 %convolution_convert_fusion = bf16[8,4,32,256]{3,0,2,1:T(8,128)(2,1)S(1)} fusion(f32[8,32,256]{2,1,0:T(8,128)} %param.6, f32[8]{0:T(128)S(1)} %dynamic_slice.23, s32[8,8]{1,0:T(8,128)S(1)} %bitcast_subtract_fusion), kind=kOutput, calls=%fused_computation.16 | convolution fusion | flops 25493760 | bytes 786720 | tf_op jit(solution)/shard_map/jas,jrv->asrv/dot_general | solution.py:119
  4.0 0.9 %copy.72 = bf16[8,4,32,256]{3,2,1,0:T(8,128)(2,1)} copy(bf16[8,4,32,256]{3,0,2,1:T(8,128)(2,1)S(1)} %convolution_convert_fusion) | data formatting | bytes 1048576 | tf_op jit(solution)/shard_map/convert_element_type | solution.py:121
  4.9 6.4 %all-to-all-start = ((bf16[8,4,32,256]{3,2,1,0:T(8,128)(2,1)}), bf16[8,4,32,256]{3,2,1,0:T(8,128)(2,1)S(1)}, u32[]{:S(2)}, u32[]{:S(2)}) async-start(bf16[8,4,32,256]{3,2,1,0:T(8,128)(2,1)} %copy.72), calls=%async_computation | async-start | bytes 1048576 | tf_op jit(solution)/shard_map/all_to_all | solution.py:120
  11.3 0.1 fusion.28
  11.4 1.3 %collective-permute-start = (bf16[1,3,11264]{2,1,0:T(4,128)(2,1)S(1)}, bf16[1,3,11264]{2,1,0:T(4,128)(2,1)S(1)}, u32[]{:S(2)}, u32[]{:S(2)}) collective-permute-start(bf16[1,3,11264]{2,1,0:T(4,128)(2,1)S(1)} %get-tuple-element.19), channel_id=1, source_target_pairs={{0,1},{1,2},{2,3},{4,5},{5,6},{6,7},{8,9},{9,10},{10,11},{12,13},{... | collective-permute-start | bytes 202760 | tf_op jit(solution)/shard_map/ppermute | solution.py:18
  12.7 1.3 %collective-permute-start.1 = (bf16[1,3,11264]{2,1,0:T(4,128)(2,1)S(1)}, bf16[1,3,11264]{2,1,0:T(4,128)(2,1)S(1)}, u32[]{:S(2)}, u32[]{:S(2)}) collective-permute-start(bf16[1,3,11264]{2,1,0:T(4,128)(2,1)S(1)} %get-tuple-element.18), channel_id=1, source_target_pairs={{1,0},{2,1},{3,2},{5,4},{6,5},{7,6},{9,8},{10,9},{11,10},{13,12},{... | collective-permute-start | bytes 202760 | tf_op jit(solution)/shard_map/ppermute | solution.py:21
  14.0 0.7 fusion.26
  14.7 0.2 dynamic-slice_reduce_fusion
  14.9 0.1 add.149
  15.0 0.1 add.150
  15.1 0.1 add.157
  15.2 0.1 convert_reduce_fusion
  15.3 0.1 select_reduce_fusion
  15.4 0.1 add.152
  15.5 0.1 add.159
  15.6 0.1 broadcast_multiply_fusion
  15.7 0.1 maximum_bitcast_fusion
  15.8 1.8 %collective-permute-done.1 = bf16[1,3,11264]{2,1,0:T(4,128)(2,1)S(1)} collective-permute-done((bf16[1,3,11264]{2,1,0:T(4,128)(2,1)S(1)}, bf16[1,3,11264]{2,1,0:T(4,128)(2,1)S(1)}, u32[]{:S(2)}, u32[]{:S(2)}) %collective-permute-start.1) | collective-permute-done | bytes 67616 | tf_op jit(solution)/shard_map/ppermute | solution.py:21
  17.6 0.1 constant_dynamic-update-slice_fusion
  17.7 0.0 collective-permute-done
  17.7 2.5 %multiply_add_fusion = f32[1,32,11264]{2,1,0:T(8,128)} fusion(bf16[1,32,11264]{2,1,0:T(8,128)(2,1)S(1)} %copy-done.1, bf16[1,3,11264]{2,1,0:T(4,128)(2,1)S(1)} %collective-permute-done, bf16[1,35,11264]{2,1,0:T(8,128)(2,1)S(1)} %constant_dynamic-update-slice_fusion), kind=kLoop, calls=%fused_computation.15 | loop fusion | flops 10452992 | bytes 4392960 | tf_op jit(solution)/shard_map/add | solution.py:38
  20.2 4.4 %all-to-all-done = bf16[8,4,32,256]{3,2,1,0:T(8,128)(2,1)S(1)} async-done(((bf16[8,4,32,256]{3,2,1,0:T(8,128)(2,1)}), bf16[8,4,32,256]{3,2,1,0:T(8,128)(2,1)S(1)}, u32[]{:S(2)}, u32[]{:S(2)}) %all-to-all-start) | async-done | bytes 524320 | tf_op jit(solution)/shard_map/all_to_all | solution.py:120
  24.6 1.1 %bitcast_convert_fusion = f32[32,32,256]{2,1,0:T(8,128)} fusion(bf16[8,4,32,256]{3,2,1,0:T(8,128)(2,1)S(1)} %all-to-all-done), kind=kLoop, calls=%fused_computation.31 | loop fusion | flops 262144 | bytes 1572864 | tf_op jit(solution)/shard_map/convert_element_type | solution.py:122
  25.7 0.3 broadcast_in_dim.11
  26.0 3.8 %scatter_fusion = f32[88,32,256]{2,1,0:T(8,128)S(1)} fusion(f32[88,32,256]{2,1,0:T(8,128)S(1)} %broadcast_in_dim.11, s32[32]{0:T(128)S(1)} %get-tuple-element.21, f32[32,32,256]{2,1,0:T(8,128)} %bitcast_convert_fusion), kind=kCustom, calls=%fused_computation.1 | custom fusion | flops 262144 | bytes 3145856 | tf_op jit(solution)/shard_map/scatter-add | solution.py:127
  29.8 0.5 convolution_bitcast_fusion.1
  30.4 0.1 slice.107
  30.5 0.2 slice_add_fusion
  30.7 0.0 copy-start
  30.8 0.8 %copy.73 = f32[1,32,88,128]{3,2,0,1:T(8,128)S(1)} copy(f32[1,32,88,128]{3,1,2,0:T(8,128)S(1)} %slice_add_fusion) | data formatting | bytes 2883584 | tf_op jit(solution)/shard_map/add | solution.py:76
  31.6 0.5 copy-done
  32.1 3.4 %fusion.11 = (bf16[4,8,88,128]{3,1,2,0:T(8,128)(2,1)S(1)}, f32[1,32,11264]{2,1,0:T(8,128)}) fusion(f32[11264]{0:T(1024)S(1)} %maximum_bitcast_fusion, f32[1,32,11264]{2,0,1:T(1,128)S(1)} %bitcast.96, f32[1,32,11264]{2,1,0:T(8,128)S(1)} %copy-done), kind=kLoop, calls=%fused_computation.30 | loop fusion | flops 6127616 | bytes 5091328
  35.5 0.1 copy.83
  35.6 0.6 convolution_bitcast_fusion
  36.2 0.2 slice.111
  36.4 0.6 fusion
  37.0 0.9 %copy.75 = f32[88,32,256]{2,1,0:T(8,128)S(1)} copy(f32[88,32,256]{2,0,1:T(8,128)S(1)} %fusion) | data formatting | bytes 5767168 | tf_op jit(solution)/shard_map/squeeze | solution.py:132
  37.9 1.6 %gather_fusion = f32[32,32,256]{2,1,0:T(8,128)} fusion(f32[88,32,256]{2,1,0:T(8,128)S(1)} %copy.75, s32[1024]{0:T(1024)S(1)} %pad_clamp_fusion), kind=kCustom, calls=%fused_computation | custom fusion | bytes 2097280 | tf_op jit(solution)/shard_map/jit(_take)/gather | solution.py:132
  39.5 2.4 %fusion.7 = f32[1,32,32,256]{3,2,0,1:T(8,128)} fusion(f32[32,32,256]{2,1,0:T(8,128)} %gather_fusion, pred[32]{0:T(512)(128)(4,1)S(1)} %compare_and_fusion), kind=kLoop, calls=%fused_computation.23 | loop fusion | flops 262144 | bytes 2097184 | tf_op jit(solution)/shard_map/jit(_take)/select_n | solution.py:132
  41.9 4.9 %all-to-all-start.1 = ((f32[1,32,32,256]{3,2,0,1:T(8,128)}), f32[1,32,32,256]{3,2,0,1:T(8,128)S(1)}, u32[]{:S(2)}, u32[]{:S(2)}) async-start(f32[1,32,32,256]{3,2,0,1:T(8,128)} %fusion.7), calls=%async_computation.1 | async-start | bytes 2097152 | tf_op jit(solution)/shard_map/all_to_all | solution.py:133
  46.8 33.5 %all-gather.1 = f32[8,1,256]{2,1,0:T(1,128)S(1)} all-gather(f32[1,1,256]{2,1,0:T(1,128)S(1)} %bitcast.99), channel_id=2, replica_groups=mesh['tile'=8,'row'=4] {'tile'}, dimensions={0}, use_global_device_ids=true | all-gather | bytes 9216 | tf_op jit(solution)/shard_map/all_gather | solution.py:96
  80.3 0.0 all-to-all-done.1
  80.3 1.5 %fusion.6 = f32[8,32,256]{2,0,1:T(8,128)S(1)} fusion(f32[8,4,32,256]{3,2,1,0:T(8,128)S(1)} %bitcast.97, f32[256]{0:T(256)S(1)} %reduce_sum.42, f32[8]{0:T(128)S(1)} %dynamic_slice.23, s32[8,8]{1,0:T(8,128)S(1)} %bitcast_subtract_fusion), kind=kOutput, calls=%fused_computation.21 | convolution fusion | flops 25297152 | bytes 1312032 | tf_op jit(solution)/shard_map/jas,asrv->jrv/dot_general | solution.py:134
  81.8 0.8 copy.78
  (16 shorter events, 0.2 us)
Async XLA Ops:
  2.3 9.0 %copy-start.1 = (bf16[1,32,11264]{2,1,0:T(8,128)(2,1)S(1)}, bf16[1,32,11264]{2,1,0:T(8,128)(2,1)}, u32[]{:S(2)}) copy-start(bf16[1,32,11264]{2,1,0:T(8,128)(2,1)} %param.5) | copy-start | bytes 2162692
  4.9 10.3 %copy-start.2 = (bf16[1,256,256]{2,1,0:T(8,128)(2,1)S(1)}, bf16[1,256,256]{2,1,0:T(8,128)(2,1)}, u32[]{:S(2)}) copy-start(bf16[1,256,256]{2,1,0:T(8,128)(2,1)} %param.7) | copy-start | bytes 393220
  4.9 19.6 %all-to-all-start = ((bf16[8,4,32,256]{3,2,1,0:T(8,128)(2,1)}), bf16[8,4,32,256]{3,2,1,0:T(8,128)(2,1)S(1)}, u32[]{:S(2)}, u32[]{:S(2)}) async-start(bf16[8,4,32,256]{3,2,1,0:T(8,128)(2,1)} %copy.72), calls=%async_computation | async-start | bytes 1048576 | tf_op jit(solution)/shard_map/all_to_all | solution.py:120
  11.4 6.3 %collective-permute-start = (bf16[1,3,11264]{2,1,0:T(4,128)(2,1)S(1)}, bf16[1,3,11264]{2,1,0:T(4,128)(2,1)S(1)}, u32[]{:S(2)}, u32[]{:S(2)}) collective-permute-start(bf16[1,3,11264]{2,1,0:T(4,128)(2,1)S(1)} %get-tuple-element.19), channel_id=1, source_target_pairs={{0,1},{1,2},{2,3},{4,5},{5,6},{6,7},{8,9},{9,10},{10,11},{12,13},{... | collective-permute-start | bytes 202760 | tf_op jit(solution)/shard_map/ppermute | solution.py:18
  12.7 4.9 %collective-permute-start.1 = (bf16[1,3,11264]{2,1,0:T(4,128)(2,1)S(1)}, bf16[1,3,11264]{2,1,0:T(4,128)(2,1)S(1)}, u32[]{:S(2)}, u32[]{:S(2)}) collective-permute-start(bf16[1,3,11264]{2,1,0:T(4,128)(2,1)S(1)} %get-tuple-element.18), channel_id=1, source_target_pairs={{1,0},{2,1},{3,2},{5,4},{6,5},{7,6},{9,8},{10,9},{11,10},{13,12},{... | collective-permute-start | bytes 202760 | tf_op jit(solution)/shard_map/ppermute | solution.py:21
  30.7 1.4 %copy-start = (f32[1,32,11264]{2,1,0:T(8,128)S(1)}, f32[1,32,11264]{2,1,0:T(8,128)}, u32[]{:S(2)}) copy-start(f32[1,32,11264]{2,1,0:T(8,128)} %multiply_add_fusion) | copy-start | bytes 4325380
  41.9 38.5 %all-to-all-start.1 = ((f32[1,32,32,256]{3,2,0,1:T(8,128)}), f32[1,32,32,256]{3,2,0,1:T(8,128)S(1)}, u32[]{:S(2)}, u32[]{:S(2)}) async-start(f32[1,32,32,256]{3,2,0,1:T(8,128)} %fusion.7), calls=%async_computation.1 | async-start | bytes 2097152 | tf_op jit(solution)/shard_map/all_to_all | solution.py:133
